TPU v7x, 32 devices: a whole 2x2x4 slice. The times are simulated.
32 devices in a mesh: leaf: 8 (over y, x, core), rows: 4 (over z).
Axes of the slice: x: 2, y: 2, z: 4, core: 2. Of those that a mesh axis runs over, the one named last changes fastest.
Arguments:
- right_side: float32 [8, 96, 2048], P('leaf', None, 'rows'), may hold values from -6 to 6
- diag_inverse: float32 [8, 2048, 2048], P('leaf', 'rows')
- lower_blocks: float32 [8, 2048, 2048], P('leaf', 'rows'), may hold values from -0.125 to 0.125
- block_pattern: int32 [8, 32, 32], P('leaf', 'rows'), may hold values 0 or 1
Outputs:
- solution: float32 [8, 96, 2048], P('leaf', None, 'rows')
- ancestor_update: float32 [8, 96, 2048], P('leaf', None, 'rows')
All inputs are finite; a program needn't handle non-finite values. No bound on the sum of `block_pattern` on one device may be relied on, other than what follows from the above.
Results may differ from a plain program's by a relative error of at most 0.00017.
Values sent between devices are 32-bit elements; how exact they have to be, the bound alone decides.
A program may use at most 64 MiB of HBM per device.

v0:
```python
import functools

import jax
import jax.numpy as jnp
from jax import lax
from jax.experimental import pallas as pl
from jax.experimental.pallas import tpu as pltpu
from jax.sharding import PartitionSpec as P

MESH = pl.DeviceIdType.MESH
WAVE = 8
AHEAD = 1
EARLY = 3
LANES = 128


def partner(place, step, size):
    if size & (size - 1):
        return (place + step) % size
    result, bit = 0, 1
    while bit < size:
        result = result + ((place // bit + step // bit) % 2) * bit
        bit *= 2
    return result


def halves(x):
    high = x.astype(jnp.bfloat16)
    low = (x - high.astype(jnp.float32)).astype(jnp.bfloat16)
    return high, low


def kernel(
    groups, splits, right_ref, inverse_hbm, lower_hbm, pattern_ref, solved_ref, update_ref,
    inverse_stage, lower_stage, inverse_parts, lower_parts, arriving, gathered, leaving, next_right,
    inverse_sem, lower_sem, arriving_sem, gathered_sem, first_sem, leaving_sem, spread_sem, right_sem,
):
    g = lax.axis_index("leaf")
    z = lax.axis_index("rows")
    waves, size, local = right_ref.shape
    width = pattern_ref.shape[1]
    pieces = inverse_sem.shape[0]
    piece = local // pieces
    total = splits * local

    def piece_copies(source, stage, sems):
        return [
            pltpu.make_async_copy(
                source.at[pl.ds(i * piece, piece)], stage.at[pl.ds(i * piece, piece)], sems.at[i]
            )
            for i in range(pieces)
        ]

    inverse_copies = piece_copies(inverse_hbm, inverse_stage, inverse_sem)
    lower_copies = piece_copies(lower_hbm, lower_stage, lower_sem)
    for copy in inverse_copies:
        copy.start()

    barrier = pltpu.get_barrier_semaphore()

    def greet(leaf, row):
        pl.semaphore_signal(
            barrier, inc=1, device_id={"leaf": leaf, "rows": row}, device_id_type=MESH
        )

    for j in range(1, splits):
        greet(g, partner(z, j, splits))

    @pl.when(g > 0)
    def _():
        for j in range(splits):
            greet(g - 1, partner(z, j, splits))

    @pl.when(g < groups - 1)
    def _():
        for j in range(splits):
            greet(g + 1, partner(z, j, splits))

    neighbours = jnp.minimum(g, 1) + jnp.minimum(groups - 1 - g, 1)
    pl.semaphore_wait(barrier, splits - 1 + splits * neighbours)

    def right_copy():
        return pltpu.make_async_remote_copy(
            src_ref=right_ref, dst_ref=next_right, send_sem=right_sem.at[0],
            recv_sem=right_sem.at[1], device_id={"leaf": g - 1, "rows": z}, device_id_type=MESH,
        )

    def first_copy(k, j):
        return pltpu.make_async_remote_copy(
            src_ref=right_ref.at[k], dst_ref=arriving.at[k, z], send_sem=first_sem.at[k, j],
            recv_sem=arriving_sem.at[k, z],
            device_id={"leaf": g, "rows": partner(z, j, splits)}, device_id_type=MESH,
        )

    def own_copy(k):
        return pltpu.make_async_copy(right_ref.at[k], arriving.at[k, z], arriving_sem.at[k, z])

    def onward_copy(k, j):
        return pltpu.make_async_remote_copy(
            src_ref=leaving.at[k], dst_ref=arriving.at[k, z], send_sem=leaving_sem.at[k, j],
            recv_sem=arriving_sem.at[k, z],
            device_id={"leaf": g + 1, "rows": partner(z, j, splits)}, device_id_type=MESH,
        )

    def spread_copy(k, j):
        return pltpu.make_async_remote_copy(
            src_ref=gathered.at[k, z], dst_ref=gathered.at[k, z], send_sem=spread_sem.at[k, j],
            recv_sem=gathered_sem.at[k, z],
            device_id={"leaf": g, "rows": partner(z, j, splits)}, device_id_type=MESH,
        )

    def first_sends(k):
        @pl.when((g == 0) & (k < waves))
        def _():
            for j in range(splits - 1, 0, -1):
                first_copy(k, j).start()
            own_copy(k).start()

    for k in range(EARLY):
        first_sends(k)

    @pl.when(g > 0)
    def _():
        right_copy().start()

    def store_turned(parts, rows, q, values):
        high, low = halves(values.T)
        parts[q, :, pl.ds(rows, piece)] = high
        parts[q, :, pl.ds(local + rows, piece)] = low

    def prepare_inverse():
        for i in range(pieces):
            inverse_copies[i].wait()
            lower_copies[i].start()
            for q in range(splits):
                store_turned(
                    inverse_parts, i * piece, q,
                    inverse_stage[pl.ds(i * piece, piece), pl.ds(q * local, local)],
                )

    def prepare_lower():
        block = total // width
        row = lax.broadcasted_iota(jnp.int32, (width, total), 0)
        column = lax.broadcasted_iota(jnp.int32, (width, total), 1)
        spread = jnp.where(column // block == row, 1.0, 0.0).astype(jnp.bfloat16)
        mask = jnp.dot(
            pattern_ref[...].astype(jnp.float32).astype(jnp.bfloat16), spread,
            preferred_element_type=jnp.float32,
        )
        for i in range(pieces):
            lower_copies[i].wait()
            for q in range(splits):
                kept = [
                    lower_stage[pl.ds(h * block, block), pl.ds(q * local, local)]
                    * mask[h : h + 1, q * local : (q + 1) * local]
                    for h in range(i * piece // block, (i + 1) * piece // block)
                ]
                store_turned(lower_parts, i * piece, q, jnp.concatenate(kept, 0))

    def product(x, parts):
        high, low = halves(x)
        out = lax.dot_general(
            jnp.concatenate([high, low], 0), parts, (((1,), (0,)), ((), ())),
            preferred_element_type=jnp.float32,
        )
        return (out[:size, :local] + (out[size:, :local] + out[:size, local:])) + out[size:, local:]

    def solve(k):
        result = None
        for j in range(splits):
            q = partner(z, j, splits)
            pltpu.make_async_copy(arriving.at[k, q], arriving.at[k, q], arriving_sem.at[k, q]).wait()
            term = product(arriving[k, q], inverse_parts[q])
            result = term if result is None else result + term
        gathered[k, z] = result
        for j in range(splits - 1, 0, -1):
            spread_copy(k, j).start()
        solved_ref[k] = result

    def push(k):
        result = None
        for j in range(splits):
            q = partner(z, j, splits)
            if j:
                pltpu.make_async_copy(gathered.at[k, q], gathered.at[k, q], gathered_sem.at[k, q]).wait()
            term = product(gathered[k, q], lower_parts[q])
            result = term if result is None else result + term

        @pl.when(g < groups - 1)
        def _():
            leaving[k] = next_right[k] - result
            for j in range(splits - 1, -1, -1):
                onward_copy(k, j).start()

        update_ref[k] = result

    prepare_inverse()

    @pl.when(g > 0)
    def _():
        prepare_lower()

    def section(k, _):
        @pl.when(k < waves)
        def _():
            solve(k)

        first_sends(k + EARLY)

        @pl.when((k == 0) & (g == 0))
        def _():
            prepare_lower()

        @pl.when((k == AHEAD) & (g < groups - 1))
        def _():
            right_copy().wait_recv()

        @pl.when(k >= AHEAD)
        def _():
            push(k - AHEAD)

        return 0

    lax.fori_loop(0, waves + AHEAD, section, 0)

    def finish(k, _):
        for j in range(1, splits):
            spread_copy(k, j).wait_send()

        @pl.when(g == 0)
        def _():
            for j in range(1, splits):
                first_copy(k, j).wait_send()

        @pl.when(g < groups - 1)
        def _():
            for j in range(splits):
                onward_copy(k, j).wait_send()

        return 0

    lax.fori_loop(0, waves, finish, 0)

    @pl.when(g > 0)
    def _():
        right_copy().wait_send()


def on_device(groups, splits, right_side, diag_inverse, lower_blocks, block_pattern):
    _, sources, local = right_side.shape
    total = diag_inverse.shape[2]
    pieces = local // LANES
    waves = sources // WAVE
    VMEM = pl.BlockSpec(memory_space=pltpu.VMEM)
    ANY = pl.BlockSpec(memory_space=pl.ANY)
    shape = jax.ShapeDtypeStruct((waves, WAVE, local), jnp.float32)
    dma = pltpu.SemaphoreType.DMA
    solved, update = pl.pallas_call(
        functools.partial(kernel, groups, splits),
        out_shape=(shape, shape),
        in_specs=[VMEM, ANY, ANY, VMEM],
        out_specs=(VMEM, VMEM),
        scratch_shapes=[
            pltpu.VMEM((local, total), jnp.float32),
            pltpu.VMEM((local, total), jnp.float32),
            pltpu.VMEM((splits, local, 2 * local), jnp.bfloat16),
            pltpu.VMEM((splits, local, 2 * local), jnp.bfloat16),
            pltpu.VMEM((waves, splits, WAVE, local), jnp.float32),
            pltpu.VMEM((waves, splits, WAVE, local), jnp.float32),
            pltpu.VMEM((waves, WAVE, local), jnp.float32),
            pltpu.VMEM((waves, WAVE, local), jnp.float32),
            dma((pieces,)),
            dma((pieces,)),
            dma((waves, splits)),
            dma((waves, splits)),
            dma((waves, splits)),
            dma((waves, splits)),
            dma((waves, splits)),
            dma((2,)),
        ],
        compiler_params=pltpu.CompilerParams(collective_id=0, has_side_effects=True),
        name="chain",
    )(
        right_side[0].reshape(waves, WAVE, local),
        diag_inverse[0],
        lower_blocks[0],
        block_pattern[0],
    )
    return solved.reshape(1, sources, local), update.reshape(1, sources, local)


def solution(mesh):
    return jax.shard_map(
        functools.partial(on_device, mesh.shape["leaf"], mesh.shape["rows"]),
        mesh=mesh,
        in_specs=(
            P("leaf", None, "rows"),
            P("leaf", "rows", None),
            P("leaf", "rows", None),
            P("leaf", "rows", None),
        ),
        out_specs=(P("leaf", None, "rows"), P("leaf", None, "rows")),
        check_vma=False,
    )
```

profile of v0, /device:TPU:7, one launch (start us, length us, event | category | flops | bytes accessed | tf_op | source)
XLA Modules:
  0.0 113.9 jit_solution(5078573280867422145)
XLA Ops:
  0.6 110.1 %chain.1 = (f32[12,8,512]{2,1,0:T(8,128)}, f32[12,8,512]{2,1,0:T(8,128)}) custom-call(f32[12,8,512]{2,1,0:T(8,128)} %bitcast.10, f32[512,2048]{1,0:T(8,128)} %bitcast.6, f32[512,2048]{1,0:T(8,128)} %bitcast.7, s32[8,32]{1,0:T(8,128)} %bitcast.11), custom_call_target="tpu_custom_call" | custom-call | tf_op jit(solution)/shard_map/chain/pallas_call | solution.py:258
  110.7 1.6 %copy.8 = f32[1,96,512]{2,1,0:T(8,128)} copy(f32[1,96,512]{2,1,0:T(8,128)} %bitcast.9) | data formatting | bytes 393216
  112.3 1.6 %copy.9 = f32[1,96,512]{2,1,0:T(8,128)} copy(f32[1,96,512]{2,1,0:T(8,128)} %bitcast.8) | data formatting | bytes 393216
where the time goes:
time: 114 us
  Pallas kernels  110 us (96%)
  local copies, waits for them, and re-layouts  3.23 us (3%)
    pallas_call x1, Pallas kernels, on_device(): pl.pallas_call(functools.partial(kernel, groups, splits), out_shape=(shap...  110 us
    unnamed x2, local copies, waits for them, and re-layouts  3.23 us

commit v1 on v0

--- a/solution.py
+++ b/solution.py
@@ -10,7 +10,10 @@
 MESH = pl.DeviceIdType.MESH
 WAVE = 8
 AHEAD = 1
+FIRST_AHEAD = 1
 EARLY = 3
+HELPER = 2
+VMEM_LIMIT = 60000000
 LANES = 128
 
 
@@ -32,8 +35,8 @@
 
 def kernel(
     groups, splits, right_ref, inverse_hbm, lower_hbm, pattern_ref, solved_ref, update_ref,
-    inverse_stage, lower_stage, inverse_parts, lower_parts, arriving, gathered, leaving, next_right,
-    inverse_sem, lower_sem, arriving_sem, gathered_sem, first_sem, leaving_sem, spread_sem, right_sem,
+    inverse_stage, lower_stage, inverse_parts, lower_parts, arriving, gathered, leaving, next_right, detour,
+    inverse_sem, lower_sem, arriving_sem, gathered_sem, first_sem, leaving_sem, spread_sem, right_sem, detour_sem, passed_sem,
 ):
     g = lax.axis_index("leaf")
     z = lax.axis_index("rows")
@@ -42,6 +45,9 @@
     pieces = inverse_sem.shape[0]
     piece = local // pieces
     total = splits * local
+    helped = groups > HELPER and splits > 1 and waves > EARLY
+    direct = EARLY if helped else waves
+    ahead = AHEAD + (FIRST_AHEAD - AHEAD) * (1 - jnp.minimum(g, 1))
 
     def piece_copies(source, stage, sems):
         return [
@@ -77,6 +83,14 @@
             greet(g + 1, partner(z, j, splits))
 
     neighbours = jnp.minimum(g, 1) + jnp.minimum(groups - 1 - g, 1)
+    if helped:
+        for one, other in ((0, HELPER), (HELPER, 0)):
+            @pl.when(g == one)
+            def _(other=other):
+                for j in range(splits):
+                    greet(other, partner(z, j, splits))
+
+        neighbours = neighbours + jnp.where((g == 0) | (g == HELPER), 1, 0)
     pl.semaphore_wait(barrier, splits - 1 + splits * neighbours)
 
     def right_copy():
@@ -109,15 +123,37 @@
             device_id={"leaf": g, "rows": partner(z, j, splits)}, device_id_type=MESH,
         )
 
-    def first_sends(k):
-        @pl.when((g == 0) & (k < waves))
-        def _():
+    def detour_copy():
+        rest = pl.ds(direct, waves - direct)
+        return pltpu.make_async_remote_copy(
+            src_ref=right_ref.at[rest], dst_ref=detour.at[rest], send_sem=detour_sem.at[0],
+            recv_sem=detour_sem.at[1], device_id={"leaf": HELPER, "rows": z}, device_id_type=MESH,
+        )
+
+    def passed_copy(k, j):
+        return pltpu.make_async_remote_copy(
+            src_ref=detour.at[k], dst_ref=arriving.at[k, z], send_sem=passed_sem.at[k, j],
+            recv_sem=arriving_sem.at[k, z],
+            device_id={"leaf": 0, "rows": partner(z, j, splits)}, device_id_type=MESH,
+        )
+
+    @pl.when(g == 0)
+    def _():
+        def direct_sends(k, _):
             for j in range(splits - 1, 0, -1):
                 first_copy(k, j).start()
+            return 0
+
+        def own_sends(k, _):
             own_copy(k).start()
-
-    for k in range(EARLY):
-        first_sends(k)
+            return 0
+
+        direct_sends(0, 0)
+        own_copy(0).start()
+        if helped:
+            detour_copy().start()
+        lax.fori_loop(1, direct, direct_sends, 0)
+        lax.fori_loop(1, waves, own_sends, 0)
 
     @pl.when(g > 0)
     def _():
@@ -196,6 +232,18 @@
 
     prepare_inverse()
 
+    if helped:
+        @pl.when(g == HELPER)
+        def _():
+            detour_copy().wait_recv()
+
+            def pass_on(k, _):
+                for j in range(splits - 1, 0, -1):
+                    passed_copy(k, j).start()
+                return 0
+
+            lax.fori_loop(direct, waves, pass_on, 0)
+
     @pl.when(g > 0)
     def _():
         prepare_lower()
@@ -205,33 +253,37 @@
         def _():
             solve(k)
 
-        first_sends(k + EARLY)
-
         @pl.when((k == 0) & (g == 0))
         def _():
             prepare_lower()
 
-        @pl.when((k == AHEAD) & (g < groups - 1))
+        @pl.when((k == ahead) & (g < groups - 1))
         def _():
             right_copy().wait_recv()
 
-        @pl.when(k >= AHEAD)
-        def _():
-            push(k - AHEAD)
+        @pl.when(k >= ahead)
+        def _():
+            push(k - ahead)
 
         return 0
 
-    lax.fori_loop(0, waves + AHEAD, section, 0)
+    lax.fori_loop(0, waves + ahead, section, 0)
 
     def finish(k, _):
         for j in range(1, splits):
             spread_copy(k, j).wait_send()
 
-        @pl.when(g == 0)
+        @pl.when((g == 0) & (k < direct))
         def _():
             for j in range(1, splits):
                 first_copy(k, j).wait_send()
 
+        if helped:
+            @pl.when((g == HELPER) & (k >= direct))
+            def _():
+                for j in range(1, splits):
+                    passed_copy(k, j).wait_send()
+
         @pl.when(g < groups - 1)
         def _():
             for j in range(splits):
@@ -244,6 +296,22 @@
     @pl.when(g > 0)
     def _():
         right_copy().wait_send()
+
+    if helped:
+        @pl.when(g == 0)
+        def _():
+            detour_copy().wait_send()
+
+
+def place(solved_ref, update_ref, solved_hbm, update_hbm, sems):
+    copies = [
+        pltpu.make_async_copy(solved_ref, solved_hbm, sems.at[0]),
+        pltpu.make_async_copy(update_ref, update_hbm, sems.at[1]),
+    ]
+    for copy in copies:
+        copy.start()
+    for copy in copies:
+        copy.wait()
 
 
 def on_device(groups, splits, right_side, diag_inverse, lower_blocks, block_pattern):
@@ -269,6 +337,7 @@
             pltpu.VMEM((waves, splits, WAVE, local), jnp.float32),
             pltpu.VMEM((waves, WAVE, local), jnp.float32),
             pltpu.VMEM((waves, WAVE, local), jnp.float32),
+            pltpu.VMEM((waves, WAVE, local), jnp.float32),
             dma((pieces,)),
             dma((pieces,)),
             dma((waves, splits)),
@@ -277,8 +346,12 @@
             dma((waves, splits)),
             dma((waves, splits)),
             dma((2,)),
+            dma((2,)),
+            dma((waves, splits)),
         ],
-        compiler_params=pltpu.CompilerParams(collective_id=0, has_side_effects=True),
+        compiler_params=pltpu.CompilerParams(
+            collective_id=0, has_side_effects=True, vmem_limit_bytes=VMEM_LIMIT
+        ),
         name="chain",
     )(
         right_side[0].reshape(waves, WAVE, local),
@@ -286,6 +359,14 @@
         lower_blocks[0],
         block_pattern[0],
     )
+    solved, update = pl.pallas_call(
+        place,
+        out_shape=(shape, shape),
+        in_specs=[VMEM, VMEM],
+        out_specs=(ANY, ANY),
+        scratch_shapes=[dma((2,))],
+        name="place",
+    )(solved, update)
     return solved.reshape(1, sources, local), update.reshape(1, sources, local)
 
 

time: 114 us -> 108 us (0.947)
  local copies, waits for them, and re-layouts: 3.23 us -> 0 us
  Pallas kernels: 110 us -> 107 us
    pallas_call x1, Pallas kernels: 110 us -> 106 us  [on_device(): pl.pallas_call(functools.partial(kernel, groups, splits), out_shape=(shap...]
    unnamed x2 -> x0, local copies, waits for them, and re-layouts: 3.23 us -> none
    pallas_call x0 -> x1, Pallas kernels: none -> 1.78 us  [on_device(): pl.pallas_call(place, out_shape=(shape, shape), in_specs=[VMEM, VMEM], ou...]
where the time goes in v1:
time: 108 us
  Pallas kernels  107 us (99%)
    pallas_call x1, Pallas kernels, on_device(): pl.pallas_call(functools.partial(kernel, groups, splits), out_shape=(shap...  106 us

profile of v1, /device:TPU:7, one launch (start us, length us, event | category | flops | bytes accessed | tf_op | source)
XLA Modules:
  0.0 108.1 jit_solution(8161657118842341197)
XLA Ops:
  0.6 105.7 %chain.1 = (f32[12,8,512]{2,1,0:T(8,128)}, f32[12,8,512]{2,1,0:T(8,128)}) custom-call(f32[12,8,512]{2,1,0:T(8,128)} %bitcast.8, f32[512,2048]{1,0:T(8,128)} %bitcast.6, f32[512,2048]{1,0:T(8,128)} %bitcast.7, s32[8,32]{1,0:T(8,128)} %bitcast.9), custom_call_target="tpu_custom_call" | custom-call | tf_op jit(solution)/shard_map/chain/pallas_call | solution.py:326
  106.3 1.8 %place.1 = (f32[12,8,512]{2,1,0:T(8,128)}, f32[12,8,512]{2,1,0:T(8,128)}) custom-call(f32[12,8,512]{2,1,0:T(8,128)} %get-tuple-element.6.solved_ref, f32[12,8,512]{2,1,0:T(8,128)} %get-tuple-element.7.update_ref), custom_call_target="tpu_custom_call" | custom-call | tf_op jit(solution)/shard_map/place/pallas_call | solution.py:362

commit v2 on v1

--- a/solution.py
+++ b/solution.py
@@ -13,7 +13,8 @@
 FIRST_AHEAD = 1
 EARLY = 3
 HELPER = 2
-VMEM_LIMIT = 60000000
+VMEM_LIMIT = 54_000_000
+PLACE_LIMIT = 4_000_000
 LANES = 128
 
 
@@ -365,6 +366,7 @@
         in_specs=[VMEM, VMEM],
         out_specs=(ANY, ANY),
         scratch_shapes=[dma((2,))],
+        compiler_params=pltpu.CompilerParams(vmem_limit_bytes=PLACE_LIMIT),
         name="place",
     )(solved, update)
     return solved.reshape(1, sources, local), update.reshape(1, sources, local)

time: 108 us -> 107 us (level)
  Pallas kernels: 107 us -> 105 us
  local copies, waits for them, and re-layouts: 0 us -> 1.61 us
    pallas_call x1, Pallas kernels: 106 us -> 104 us  [on_device(): pl.pallas_call(functools.partial(kernel, groups, splits), out_shape=(shap...]
    unnamed x0 -> x4, local copies, waits for them, and re-layouts: none -> 1.61 us
where the time goes in v2:
time: 107 us
  Pallas kernels  105 us (98%)
  local copies, waits for them, and re-layouts  1.61 us (2%)
    pallas_call x1, Pallas kernels, on_device(): pl.pallas_call(functools.partial(kernel, groups, splits), out_shape=(shap...  104 us

profile of v2, /device:TPU:7, one launch (start us, length us, event | category | flops | bytes accessed | tf_op | source)
XLA Modules:
  0.0 107.0 jit_solution(14112559662496485369)
XLA Ops:
  0.6 0.0 copy-start
  0.6 0.9 copy-done
  1.6 0.0 copy-start.1
  1.6 0.7 copy-done.1
  2.2 104.0 %chain.1 = (f32[12,8,512]{2,1,0:T(8,128)S(1)}, f32[12,8,512]{2,1,0:T(8,128)S(1)}) custom-call(f32[12,8,512]{2,1,0:T(8,128)S(1)} %bitcast.6, f32[512,2048]{1,0:T(8,128)} %bitcast.8, f32[512,2048]{1,0:T(8,128)} %bitcast.9, s32[8,32]{1,0:T(8,128)S(1)} %bitcast.7), custom_call_target="tpu_custom_call" | custom-call | tf_op jit(solution)/shard_map/chain/pallas_call | solution.py:327
  106.3 0.8 place.1
Async XLA Ops:
  0.6 0.9 copy-start
  1.6 0.7 copy-start.1

commit v3 on v2

--- a/solution.py
+++ b/solution.py
@@ -13,7 +13,7 @@
 FIRST_AHEAD = 1
 EARLY = 3
 HELPER = 2
-VMEM_LIMIT = 54_000_000
+VMEM_LIMIT = 56_000_000
 PLACE_LIMIT = 4_000_000
 LANES = 128
 
@@ -327,7 +327,7 @@
     solved, update = pl.pallas_call(
         functools.partial(kernel, groups, splits),
         out_shape=(shape, shape),
-        in_specs=[VMEM, ANY, ANY, VMEM],
+        in_specs=[ANY, ANY, ANY, VMEM],
         out_specs=(VMEM, VMEM),
         scratch_shapes=[
             pltpu.VMEM((local, total), jnp.float32),

time: 107 us -> 106 us (level)
  no operation moved by 1% of the time
where the time goes in v3:
time: 106 us
  Pallas kernels  105 us (99%)
    pallas_call x1, Pallas kernels, on_device(): pl.pallas_call(functools.partial(kernel, groups, splits), out_shape=(shap...  104 us

profile of v3, /device:TPU:7, one launch (start us, length us, event | category | flops | bytes accessed | tf_op | source)
XLA Modules:
  0.0 106.3 jit_solution(12710702737727286595)
XLA Ops:
  0.6 0.0 copy-start
  0.6 0.7 copy-done
  1.3 104.2 %chain.1 = (f32[12,8,512]{2,1,0:T(8,128)S(1)}, f32[12,8,512]{2,1,0:T(8,128)S(1)}) custom-call(f32[12,8,512]{2,1,0:T(8,128)} %bitcast.9, f32[512,2048]{1,0:T(8,128)} %bitcast.7, f32[512,2048]{1,0:T(8,128)} %bitcast.8, s32[8,32]{1,0:T(8,128)S(1)} %bitcast.6), custom_call_target="tpu_custom_call" | custom-call | tf_op jit(solution)/shard_map/chain/pallas_call | solution.py:327
  105.5 0.8 place.1
Async XLA Ops:
  0.6 0.7 copy-start
